TPU v7x, 32 devices: a whole 2x2x4 slice. The times are simulated.
32 devices in a mesh: seq: 8 (over y, x, core), head: 4 (over z).
Axes of the slice: x: 2, y: 2, z: 4, core: 2. Of those that a mesh axis runs over, the one named last changes fastest.
Arguments:
- inputs: bfloat16 [2048, 4096], P('seq'), may hold values from -6 to 6
- x_weight: bfloat16 [4096, 8192], P('seq', 'head'), may hold values from -0.125 to 0.125
- b_values: bfloat16 [2048, 8, 128], P('seq'), may hold values from -0.5 to 0.5
- c_values: bfloat16 [2048, 8, 128], P('seq'), may hold values from -0.375 to 0.375
- gate_z: bfloat16 [2048, 8192], P('seq', 'head'), may hold values from -6 to 6
- log_decay: float32 [2048, 128], P('seq', 'head'), may hold values from -2 to 0
- skip_gain: float32 [128], P('head'), may hold values from 0.5 to 1.5
- grad_out: bfloat16 [2048, 8192], P('seq', 'head'), may hold values from -6 to 6
Outputs:
- input_grad: bfloat16 [2048, 4096], P('seq', 'head')
- z_grad: bfloat16 [2048, 8192], P('seq', 'head')
All inputs are finite; a program needn't handle non-finite values.
Results may differ from a plain program's by a relative error of at most 0.0095.
Values may be sent and summed in bfloat16 or wider, within the bound.
A program may use at most 128 MiB of HBM per device.

v0:
```python
import jax
import jax.numpy as jnp
from jax import lax
from jax.sharding import PartitionSpec as P

HEADS = 128
HEAD_DIM = 64
STATE = 128
GROUPS = 8
SPAN = 256


EXACT_MODE = lax.Precision.HIGHEST


def prefix_2(array, axis, combine, identity):
    size, place = (lax.axis_size(axis), lax.axis_index(axis))
    everything = jax.tree.map(
        lambda part, kind: lax.all_gather(part.astype(kind), axis),
        array,
        (jnp.bfloat16, jnp.bfloat16),
    )
    start = jax.tree.map(
        lambda part, zero: jnp.broadcast_to(jnp.asarray(zero, part.dtype), part.shape),
        array,
        identity,
    )

    def prefix_hop(k, before):
        reached = k < place
        new = combine(
            before, jax.tree.map(lambda part, own: part[k].astype(own.dtype), everything, array)
        )
        return jax.tree.map(lambda a, b: jnp.where(reached, a, b), new, before)

    return lax.fori_loop(0, size, prefix_hop, start)


def entering(value, axis, join, neutral):
    count, mine = (lax.axis_size(axis), lax.axis_index(axis))
    pieces = jax.tree.map(lambda part: lax.all_gather(part, axis), value)
    pieces = jax.tree.map(lambda part: part[::-1], pieces)
    mine = count - 1 - mine
    so_far = jax.tree.map(
        lambda part, zero: jnp.full_like(part, 0) + jnp.asarray(zero, part.dtype), value, neutral
    )

    def entering_hop(position, so_far):
        longer = join(so_far, jax.tree.map(lambda part: part[position], pieces))
        return jax.tree.map(lambda new, old: jnp.where(position < mine, new, old), longer, so_far)

    return lax.fori_loop(0, count - 1, entering_hop, so_far)


def decayed_scores(c_block, b_block, prefix):
    scores = jnp.einsum("thn,shn->hts", c_block, b_block, preferred_element_type=jnp.float32)
    later = prefix.T[:, :, None]
    earlier = prefix.T[:, None, :]
    positions = jnp.arange(prefix.shape[0])
    causal = (positions[:, None] >= positions[None, :])[None, :, :]
    spacing = jnp.where(causal, later - earlier, 0.0)
    factors = jnp.where(causal, jnp.exp(spacing), 0.0)
    return (scores * factors).astype(jnp.bfloat16)


def compose(earlier, later):
    return (earlier[0] * later[0], later[0][:, None, None] * earlier[1] + later[1])


def body(inputs, x_weight, b_values, c_values, gate_z, log_decay, skip_gain, grad_out):
    token_count = inputs.shape[0]
    head_count = log_decay.shape[1]
    width_here = x_weight.shape[1]
    block_count = token_count // SPAN
    full_weight = lax.all_gather(x_weight, "seq", axis=0, tiled=True)
    x_sums = jnp.dot(inputs, full_weight, preferred_element_type=jnp.float32)
    x_values = x_sums.astype(jnp.bfloat16)
    first_head = lax.axis_index("head") * head_count
    owners = (first_head + jnp.arange(head_count)) // (HEADS // GROUPS)
    picker = (owners[:, None] == jnp.arange(GROUPS)[None, :]).astype(jnp.bfloat16)
    b_heads = jnp.einsum(
        "tgn,hg->thn", b_values, picker, preferred_element_type=jnp.float32
    ).astype(jnp.bfloat16)
    c_heads = jnp.einsum(
        "tgn,hg->thn", c_values, picker, preferred_element_type=jnp.float32
    ).astype(jnp.bfloat16)
    x_blocks = x_values.reshape(block_count, SPAN, head_count, HEAD_DIM)
    b_blocks = b_heads.reshape(block_count, SPAN, head_count, STATE)
    c_blocks = c_heads.reshape(block_count, SPAN, head_count, STATE)
    prefix = jnp.cumsum(log_decay.reshape(block_count, SPAN, head_count), axis=1)
    totals = prefix[:, -1, :]
    gate = gate_z.astype(jnp.float32).reshape(token_count, head_count, HEAD_DIM)
    upstream = grad_out.astype(jnp.float32).reshape(token_count, head_count, HEAD_DIM)
    sigma = jax.nn.sigmoid(gate)
    y_grad = upstream * gate * sigma
    grad_blocks = y_grad.reshape(block_count, SPAN, head_count, HEAD_DIM)
    low_blocks = grad_blocks.astype(jnp.bfloat16)
    tails = jnp.exp(totals[:, None, :] - prefix)
    fresh_states = jnp.einsum(
        "kshp,kshn->khpn",
        x_blocks.astype(jnp.float32) * tails[..., None],
        b_blocks.astype(jnp.float32),
        precision=EXACT_MODE,
    )
    fresh_grads = jnp.einsum(
        "kthp,kthn->khpn",
        grad_blocks * jnp.exp(prefix)[..., None],
        c_blocks.astype(jnp.float32),
        precision=EXACT_MODE,
    )
    running = jnp.cumsum(totals, axis=0)
    after = running[-1][None, :] - running
    before = running - totals
    device_decay = jnp.exp(running[-1])
    device_state = jnp.einsum("kh,khpn->hpn", jnp.exp(after), fresh_states, precision=EXACT_MODE)
    device_grad = jnp.einsum("kh,khpn->hpn", jnp.exp(before), fresh_grads, precision=EXACT_MODE)
    unit_decay = jnp.ones((head_count,), jnp.float32)
    start_state = prefix_2(
        (device_decay, device_state), "seq", compose, (unit_decay, jnp.zeros_like(device_state))
    )[1]
    end_grad = entering(
        (device_decay, device_grad), "seq", compose, (unit_decay, jnp.zeros_like(device_grad))
    )[1]
    gain = skip_gain[None, :, None]

    def forward(state, items):
        x_block, b_block, c_block, prefix_block, fresh = items
        weights = decayed_scores(c_block, b_block, prefix_block)
        local = jnp.einsum("hts,shp->thp", weights, x_block, preferred_element_type=jnp.float32)
        carried = jnp.exp(prefix_block)[:, :, None] * jnp.einsum(
            "thn,hpn->thp", c_block.astype(jnp.float32), state, precision=EXACT_MODE
        )
        state = jnp.exp(prefix_block[-1])[:, None, None] * state + fresh
        return (state, (local + carried + gain * x_block.astype(jnp.float32), weights))

    final_state, (outputs, weight_blocks) = lax.scan(
        forward, start_state, (x_blocks, b_blocks, c_blocks, prefix, fresh_states)
    )
    outputs = outputs.reshape(token_count, head_count, HEAD_DIM)
    z_grad = (upstream * outputs * sigma * (1.0 + gate * (1.0 - sigma))).astype(jnp.bfloat16)
    z_grad = z_grad.reshape(token_count, width_here)

    def backward(carry, items):
        weights, b_block, tail_block, total_block, grad_block, low_block, fresh = items
        local = jnp.einsum("hts,thp->shp", weights, low_block, preferred_element_type=jnp.float32)
        carried = tail_block[:, :, None] * jnp.einsum(
            "shn,hpn->shp", b_block.astype(jnp.float32), carry, precision=EXACT_MODE
        )
        carry = jnp.exp(total_block)[:, None, None] * carry + fresh
        return (carry, local + carried + gain * grad_block)

    final_grad, x_grads = lax.scan(
        backward,
        end_grad,
        (weight_blocks, b_blocks, tails, totals, grad_blocks, low_blocks, fresh_grads),
        reverse=True,
    )
    x_grad = x_grads.reshape(token_count, width_here).astype(jnp.bfloat16)
    partial_sums = jnp.einsum("tk,dk->td", x_grad, full_weight, preferred_element_type=jnp.float32)
    input_grad = lax.psum_scatter(
        partial_sums.astype(jnp.bfloat16), "head", scatter_dimension=1, tiled=True
    )
    return (input_grad, z_grad)


def solution(mesh):
    in_specs = (
        P("seq", None),
        P("seq", "head"),
        P("seq", None, None),
        P("seq", None, None),
        P("seq", "head"),
        P("seq", "head"),
        P("head"),
        P("seq", "head"),
    )
    out_specs = (P("seq", "head"), P("seq", "head"))
    return jax.shard_map(body, mesh=mesh, in_specs=in_specs, out_specs=out_specs, check_vma=False)
```

profile of v0, /device:TPU:16, one launch (start us, length us, event | category | flops | bytes accessed | tf_op | source)
XLA Modules:
  0.0 321.9 jit_solution(4623977196892682287)
XLA Ops:
  9.8 2.0 convert_bitcast_fusion
  11.9 89.0 %all-gather.8.cloned.1.call-done = bf16[4096,2048]{1,0:T(8,128)(2,1)} async-done(((bf16[512,2048]{1,0:T(8,128)(2,1)}), bf16[4096,2048]{1,0:T(8,128)(2,1)}) %all-gather.8.cloned.1.call-update) | async-done | bytes 16777232 | tf_op jit(solution)/shard_map/all_gather | solution.py:75
  100.9 8.3 %convolution_convert_fusion.1 = bf16[256,2048]{1,0:T(8,128)(2,1)S(1)} fusion(bf16[256,4096]{1,0:T(8,128)(2,1)S(1)} %copy-done, bf16[4096,2048]{1,0:T(8,128)(2,1)} %all-gather.8.cloned.1.call-done), kind=kOutput, calls=%fused_computation.14 | convolution fusion | flops 4295491584 | bytes 19922944 | tf_op jit(solution)/shard_map/dot_general | solution.py:76
  109.9 4.3 %fusion.32 = bf16[32,64,128]{2,1,0:T(8,128)(2,1)} fusion(bf16[256,32,128]{2,1,0:T(8,128)(2,1)} %convert_bitcast_fusion, bf16[256,32,64]{0,2,1:T(8,128)(2,1)S(1)} %bitcast.101, f32[256,32]{0,1:T(8,128)S(1)} %copy-done.8, f32[32]{0:T(128)S(1)} %subtract_exponential_fusion), kind=kOutput, calls=%fused_computation.43 | convolution fusion | flops 806879232 | bytes 3702912 | tf_op jit(solution)/shard_map/kshp,kshn->khpn/dot_general | solution.py:99
  114.4 8.9 %all-gather.3 = bf16[8,1,32]{2,1,0:T(2,128)(2,1)S(1)} all-gather(bf16[1,1,32]{2,1,0:T(2,128)(2,1)S(1)} %get-tuple-element.325), channel_id=5, replica_groups=mesh['seq'=8,'head'=4] {'seq'}, dimensions={0}, use_global_device_ids=true | all-gather | bytes 576 | tf_op jit(solution)/shard_map/all_gather | solution.py:19
  125.0 6.0 %multiply_convert_fusion = bf16[32,256,256]{2,1,0:T(8,128)(2,1)S(1)} fusion(f32[32,256]{1,0:T(8,128)S(1)} %copy.73, pred[256,256]{1,0:T(8,128)(4,1)S(1)} %iota_compare_fusion, bf16[256,32,128]{2,1,0:T(8,128)(2,1)S(1)} %copy-done.4, bf16[256,32,128]{2,1,0:T(8,128)(2,1)S(1)} %convert_bitcast_fusion.1), kind=kOutput, calls=%fused_computation.6 | convolution fusion | flops 547356672 | bytes 8486912 | tf_op jit(solution)/shard_map/while/body/eval_jaxpr/thn,shn->hts/dot_general | solution.py:56
  131.0 2.0 copy-done.3
  133.0 2.7 fusion.45
  135.7 15.4 %all-gather.12.cloned.1.call-done = bf16[256,64,128]{2,1,0:T(8,128)(2,1)} async-done(((bf16[32,64,128]{2,1,0:T(8,128)(2,1)}), bf16[256,64,128]{2,1,0:T(8,128)(2,1)}) %all-gather.12.cloned.1.call-update) | async-done | bytes 4194320 | tf_op jit(solution)/shard_map/all_gather | solution.py:19
  151.1 10.7 %while.19 = (s32[]{:T(128)}, f32[32,64,128]{2,1,0:T(8,128)S(1)}, s32[]{:T(128)}, bf16[8,32]{1,0:T(8,128)(2,1)S(1)}, bf16[8,32,64,128]{3,2,1,0:T(8,128)(2,1)}, /*index=5*/s32[]{:T(128)}, s32[]{:T(128)}) while((s32[]{:T(128)}, f32[32,64,128]{2,1,0:T(8,128)S(1)}, s32[]{:T(128)}, bf16[8,32]{1,0:T(8,128)(2,1)S(1)}, ...), condition=%wide.region_6.7_spmd.clone, body=%wide.region_5.6_spmd.clone.sunk | while | flops 1310756 | bytes 2621873 | solution.py:36
  155.2 1.3 fusion.61
  159.2 1.3 fusion.61
  161.8 6.3 %fusion.6 = f32[256,32,64]{0,2,1:T(8,128)} fusion(bf16[256,32,64]{0,2,1:T(8,128)(2,1)S(1)} %bitcast.103, f32[32,64,256]{2,1,0:T(8,128)} %fusion.45, f32[32,64,128]{2,1,0:T(8,128)S(1)} %get-tuple-element.254, bf16[256,32,128]{2,1,0:T(8,128)(2,1)} %copy-done.2, f32[256,32]{0,1:T(8,128)S(1)} %copy.80, f32[32]{0:T(128)S(1)} %copy-done.11), kind=kOutput, calls=%fused_computation.19 | convolution fusion | flops 807927808 | bytes 8421504 | tf_op jit(solution)/shard_map/while/body/eval_jaxpr/thn,hpn->thp/dot_general | solution.py:130
  168.2 2.0 copy.83
  170.2 3.9 %fusion.4 = (bf16[256,2048]{1,0:T(8,128)(2,1)}, f32[256,2048]{1,0:T(8,128)}) fusion(f32[256,2048]{1,0:T(8,128)S(1)} %copy.83, bf16[256,2048]{1,0:T(8,128)(2,1)S(1)} %copy-done.5, bf16[256,2048]{1,0:T(8,128)(2,1)} %param.16), kind=kLoop, calls=%fused_computation.17 | loop fusion | flops 7340032 | bytes 7340032 | tf_op jit(solution)/shard_map/convert_element_type | solution.py:140
  174.1 1.9 copy.67
  176.0 4.5 %fusion.24 = f32[32,64,128]{2,1,0:T(8,128)} fusion(bf16[256,32,128]{2,1,0:T(8,128)(2,1)} %copy-done.2, f32[256,32,64]{0,2,1:T(8,128)S(1)} %bitcast.98, f32[256,32]{0,1:T(8,128)S(1)} %copy.76, f32[32]{0:T(128)S(1)} %subtract_exponential_fusion), kind=kOutput, calls=%fused_computation.41 | convolution fusion | flops 806092800 | bytes 5275776 | tf_op jit(solution)/shard_map/kthp,kthn->khpn/dot_general | solution.py:105
  180.6 8.9 %all-gather = f32[8,1,32]{2,1,0:T(1,128)S(1)} all-gather(f32[1,1,32]{2,1,0:T(1,128)S(1)} %get-tuple-element.327), channel_id=2, replica_groups=mesh['seq'=8,'head'=4] {'seq'}, dimensions={0}, use_global_device_ids=true | all-gather | bytes 1152 | tf_op jit(solution)/shard_map/all_gather | solution.py:41
  189.6 4.6 %fusion.37 = f32[32,64,256]{2,1,0:T(8,128)} fusion(bf16[32,256,256]{2,1,0:T(8,128)(2,1)} %copy-done.3, f32[256,32,64]{0,2,1:T(8,128)S(1)} %bitcast.99), kind=kOutput, calls=%fused_computation.46 | convolution fusion | flops 268959744 | bytes 8388608 | tf_op jit(solution)/shard_map/while/body/eval_jaxpr/hts,thp->shp/dot_general | solution.py:145
  194.2 40.9 %all-gather.10.cloned.1.call-done = f32[256,64,128]{2,1,0:T(8,128)} async-done(((f32[32,64,128]{2,1,0:T(8,128)}), f32[256,64,128]{2,1,0:T(8,128)}) %all-gather.10.cloned.1.call-update) | async-done | bytes 8388624 | tf_op jit(solution)/shard_map/all_gather | solution.py:41
  235.1 8.3 %rev.7 = f32[8,32,64,128]{3,2,1,0:T(8,128)} reverse(f32[8,32,64,128]{3,2,1,0:T(8,128)} %bitcast.104), dimensions={0} | reverse | bytes 16777216 | tf_op jit(solution)/shard_map/rev | solution.py:42
  243.4 10.5 %while.18 = (s32[]{:T(128)}, f32[32,64,128]{2,1,0:T(8,128)S(1)}, s32[]{:T(128)}, f32[8,32]{1,0:T(8,128)S(1)}, f32[8,32,64,128]{3,2,1,0:T(8,128)}, /*index=5*/s32[]{:T(128)}, s32[]{:T(128)}) while((s32[]{:T(128)}, f32[32,64,128]{2,1,0:T(8,128)S(1)}, s32[]{:T(128)}, f32[8,32]{1,0:T(8,128)S(1)}, f32[8,32,64,128]{3,2,1,0:T(8,128)}, ...), condition=%wide.region_3.4_spmd.clone, body=%wide.region_2.3_spmd.clone.sunk | while | flops 1048580 | bytes 3146225 | solution.py:52
  243.4 1.5 fusion.60
  244.9 1.5 fusion.60
  246.4 1.5 fusion.60
  247.9 1.5 fusion.60
  249.4 1.5 fusion.60
  250.9 1.5 fusion.60
  252.5 1.5 fusion.60
  253.9 5.9 %fusion.15 = bf16[256,32,64]{0,2,1:T(8,128)(2,1)} fusion(f32[32,64,256]{2,1,0:T(8,128)} %fusion.37, f32[256,32,64]{0,2,1:T(8,128)S(1)} %bitcast.100, f32[32,64,128]{2,1,0:T(8,128)S(1)} %get-tuple-element.253, bf16[256,32,128]{2,1,0:T(8,128)(2,1)} %convert_bitcast_fusion, f32[32]{0:T(128)S(1)} %copy-done.11, f32[256,32]{0,1:T(8,128)S(1)} %copy-done.9), kind=kOutput, calls=%fused_computation.30 | convolution fusion | flops 807927808 | bytes 8421504 | tf_op jit(solution)/shard_map/while/body/eval_jaxpr/shn,hpn->shp/dot_general | solution.py:146
  259.9 12.1 %convolution_convert_fusion = bf16[256,4096]{1,0:T(8,128)(2,1)} fusion(bf16[256,2048]{0,1:T(8,128)(2,1)} %bitcast.110, bf16[4096,2048]{1,0:T(8,128)(2,1)} %all-gather.8.cloned.1.call-done), kind=kOutput, calls=%fused_computation.7 | convolution fusion | flops 4296015872 | bytes 19922944 | tf_op jit(solution)/shard_map/tk,dk->td/dot_general | solution.py:159
  272.0 43.4 %reduce-scatter.2.cloned.1.call-done = bf16[256,1024]{1,0:T(8,128)(2,1)} async-done(((bf16[256,4096]{1,0:T(8,128)(2,1)}), bf16[256,1024]{1,0:T(8,128)(2,1)}) %reduce-scatter.2.cloned.1.call-update) | async-done | bytes 524304 | tf_op jit(solution)/shard_map/reduce_scatter | solution.py:160
  (75 shorter events, 13.2 us)
Async XLA Ops:
  7.2 93.7 %copy-start = (bf16[256,4096]{1,0:T(8,128)(2,1)S(1)}, bf16[256,4096]{1,0:T(8,128)(2,1)}, u32[]{:S(2)}) copy-start(bf16[256,4096]{1,0:T(8,128)(2,1)} %param.12) | copy-start | bytes 6291460
  7.2 0.9 copy-start.10
  7.2 2.6 copy-start.6
  7.2 93.7 %all-gather.8.cloned.1.call-start = ((), (), s32[]{:S(2)}) async-start(), calls=%async_computation.1 | async-start | bytes 18874368 | tf_op jit(solution)/shard_map/all_gather | solution.py:75
  7.9 143.2 %all-gather.12.cloned.1.call-start = ((), (), s32[]{:S(2)}) async-start(), calls=%async_computation.4 | async-start | bytes 4718592 | tf_op jit(solution)/shard_map/all_gather | solution.py:19
  109.2 0.8 copy-start.8
  109.9 13.5 %copy-start.7 = (bf16[256,8,128]{2,1,0:T(8,128)(2,1)S(1)}, bf16[256,8,128]{2,1,0:T(8,128)(2,1)}, u32[]{:S(2)}) copy-start(bf16[256,8,128]{2,1,0:T(8,128)(2,1)} %param.15) | copy-start | bytes 1572868
  114.3 120.9 %all-gather.10.cloned.1.call-start = ((), (), s32[]{:S(2)}) async-start(), calls=%async_computation.3 | async-start | bytes 9437184 | tf_op jit(solution)/shard_map/all_gather | solution.py:41
  123.4 1.6 copy-start.4
  125.0 6.0 %copy-start.2 = (bf16[256,32,128]{2,1,0:T(8,128)(2,1)}, bf16[256,32,128]{2,1,0:T(8,128)(2,1)S(1)}, u32[]{:S(2)}) copy-start(bf16[256,32,128]{2,1,0:T(8,128)(2,1)S(1)} %convert_bitcast_fusion.1) | copy-start | bytes 6291460
  131.0 2.0 copy-start.3
  151.1 10.7 %copy-start.11 = (f32[32]{0:T(128)S(1)}, f32[32]{0:T(128)}, u32[]{:S(2)}) copy-start(f32[32]{0:T(128)} %param.18) | copy-start | bytes 388
  168.2 2.0 copy-start.5
  180.6 134.8 %reduce-scatter.2.cloned.1.call-start = ((), (), s32[]{:S(2)}) async-start(), calls=%async_computation.2 | async-start | bytes 2621440 | tf_op jit(solution)/shard_map/reduce_scatter | solution.py:160
  243.4 10.5 %copy-start.9 = (f32[256,32]{0,1:T(8,128)S(1)}, f32[256,32]{0,1:T(8,128)}, u32[]{:S(2)}) copy-start(f32[256,32]{0,1:T(8,128)} %copy.75) | copy-start | bytes 98308
  259.9 55.5 %copy-start.1 = (bf16[256,4096]{1,0:T(8,128)(2,1)S(1)}, bf16[256,4096]{1,0:T(8,128)(2,1)}, u32[]{:S(2)}) copy-start(bf16[256,4096]{1,0:T(8,128)(2,1)} %param.12) | copy-start | bytes 6291460
Sparse Core Ops, SparseCore 0:
  9.9 90.9 all-gather.7
  114.4 36.7 all-gather.11
  180.7 54.3 all-gather.9
  272.1 43.1 reduce-scatter.1
where the time goes:
time: 325 us; the launch traced here: 322 us
  waiting for transfers between devices  189 us (58%)
  matrix products  57.6 us (18%)
  other arithmetic  25.4 us (8%)
  blocking collectives  17.8 us (5%)
  local copies, waits for them, and re-layouts  17.1 us (5%)
  between operations  14 us (4%)
    all_gather x1, waiting for transfers between devices, body(): full_weight = lax.all_gather(x_weight, 'seq', axis=0, tiled=True)  89 us
    reduce_scatter x1, waiting for transfers between devices, body(): lax.psum_scatter(partial_sums.astype(jnp.bfloat16), 'head', scatter_dimen...  43.4 us
    all_gather x1, waiting for transfers between devices, entering(): pieces = jax.tree.map(lambda part: lax.all_gather(part, axis), value)  40.9 us
    all_gather x1, waiting for transfers between devices, prefix_2(): lax.all_gather(part.astype(kind), axis)  15.4 us
    dot_general x1, matrix products, body(): jnp.einsum('tk,dk->td', x_grad, full_weight, preferred_element_type=jnp.f...  12.1 us
    select_n x8, other arithmetic, prefix_hop(): return jax.tree.map(lambda a, b: jnp.where(reached, a, b), new, before)  10.4 us
    select_n x7, other arithmetic, entering_hop(): jnp.where(position < mine, new, old)  10.3 us
    all_gather x1, blocking collectives, entering(): pieces = jax.tree.map(lambda part: lax.all_gather(part, axis), value)  8.93 us
  transfers between devices with their start and end apart: 4, of which 4 were waited for; matrix products, arithmetic and copies ran while one was open for 6% of the time, Pallas kernels for 0%

commit v1 on v0

--- a/solution.py
+++ b/solution.py
@@ -2,6 +2,8 @@
 import jax.numpy as jnp
 from jax import lax
 from jax.sharding import PartitionSpec as P
+from jax.experimental import pallas as pl
+from jax.experimental.pallas import tpu as pltpu
 
 HEADS = 128
 HEAD_DIM = 64
@@ -163,6 +165,381 @@
     return (input_grad, z_grad)
 
 
+SEQ = 8
+RUNS = 4
+F32 = jnp.float32
+BF16 = jnp.bfloat16
+
+
+def dot_nn(a, b):
+    return lax.dot_general(a, b, (((1,), (0,)), ((), ())), preferred_element_type=F32)
+
+
+def dot_nt(a, b):
+    return lax.dot_general(a, b, (((1,), (1,)), ((), ())), preferred_element_type=F32)
+
+
+def dot_tn(a, b):
+    return lax.dot_general(a, b, (((0,), (0,)), ((), ())), preferred_element_type=F32)
+
+
+def mixer_kernel(
+    inputs, w_hbm, b2, c2, gz, go, pexp, prow, gain, tt,
+    out_ref, zg_ref,
+    wbuf, xacc, xg, xg16, ysc, wts, gmat, x16, pbuf, rsbuf,
+    fbuf, rf, sb, rr, rt,
+    wsend, wrecv, wlocal, tsend, trecv, esend, erecv, rsend, rrecv,
+):
+    s = lax.axis_index("seq")
+    z = lax.axis_index("head")
+    core, xx, yy = s % 2, (s // 2) % 2, s // 4
+    half = w_hbm.shape[1]
+    heads = wts.shape[0]
+    pairs = heads // 2
+    per_group = pairs // b2.shape[0]
+
+    def peer(r):
+        a = (1 - core) if r & 1 else core
+        b = (1 - xx) if r & 2 else xx
+        c = (1 - yy) if r & 4 else yy
+        return c * 4 + b * 2 + a
+
+    def peer_dyn(r):
+        a = (core + r) % 2
+        b = (xx + r // 2) % 2
+        c = (yy + r // 4) % 2
+        return c * 4 + b * 2 + a
+
+    barrier = pltpu.get_barrier_semaphore()
+    for r in range(1, SEQ):
+        pl.semaphore_signal(barrier, inc=1, device_id={"seq": peer(r)}, device_id_type=pl.DeviceIdType.MESH)
+    for dz in range(1, RUNS):
+        pl.semaphore_signal(barrier, inc=1, device_id={"head": (z + dz) % RUNS}, device_id_type=pl.DeviceIdType.MESH)
+    pl.semaphore_wait(barrier, SEQ - 1 + RUNS - 1)
+
+    def wcopy(src_slot, dst_slot, h, to):
+        src = w_hbm.at[h] if src_slot == 0 else wbuf.at[src_slot, h]
+        return pltpu.make_async_remote_copy(
+            src_ref=src, dst_ref=wbuf.at[dst_slot, h],
+            send_sem=wsend.at[dst_slot, h], recv_sem=wrecv.at[dst_slot, h],
+            device_id={"seq": peer(to)}, device_id_type=pl.DeviceIdType.MESH)
+
+    own = pltpu.make_async_copy(w_hbm, wbuf.at[0], wlocal)
+    sent = []
+
+    def go_send(src_slot, dst_slot, h, to):
+        cp = wcopy(src_slot, dst_slot, h, to)
+        cp.start()
+        sent.append(cp)
+
+    def w_wait(slot, h, to):
+        wcopy(0, slot, h, to).wait_recv()
+
+    def tcopy(r, slot):
+        k = peer(r)
+        return pltpu.make_async_remote_copy(
+            src_ref=tt.at[k], dst_ref=rt.at[slot], send_sem=tsend.at[r], recv_sem=trecv.at[slot],
+            device_id={"seq": k}, device_id_type=pl.DeviceIdType.MESH)
+
+    for r in range(1, SEQ):
+        tcopy(r, s).start()
+    go_send(0, 2, 0, 2)
+    go_send(0, 4, 1, 4)
+    go_send(0, 2, 1, 2)
+    go_send(0, 4, 0, 4)
+    own.start()
+    go_send(0, 1, 0, 1)
+    go_send(0, 1, 1, 1)
+
+    rt[s] = tt[s]
+    for g in range(b2.shape[0]):
+        gmat[g] = dot_nt(c2[g], b2[g])
+    xacc[...] = jnp.zeros_like(xacc)
+    lanes = lax.broadcasted_iota(jnp.int32, (SPAN, 128), 1)
+    left = lanes < HEAD_DIM
+    causal = lax.broadcasted_iota(jnp.int32, (SPAN, SPAN), 0) >= lax.broadcasted_iota(jnp.int32, (SPAN, SPAN), 1)
+
+    def columns_of(i):
+        return pl.ds(pl.multiple_of(i * 128, 128), 128)
+
+    def back_pair(i, carry):
+        cols = columns_of(i)
+        gate = gz[:, cols].astype(F32)
+        up = go[:, cols].astype(F32)
+        grad = up * gate * jax.nn.sigmoid(gate)
+        low = grad.astype(BF16)
+        pe = pexp[i]
+        ysc[:, cols] = (grad * jnp.exp(pe)).astype(BF16)
+        scores = gmat[i // per_group]
+        acc = []
+        for k in range(2):
+            later = pe[:, HEAD_DIM * k:HEAD_DIM * k + 1]
+            earlier = prow[i, k:k + 1, :]
+            factors = jnp.exp(jnp.where(causal, later - earlier, -1e30))
+            w = (scores * factors).astype(BF16)
+            wts[2 * i + k] = w
+            acc.append(dot_tn(w, low))
+        xg[:, cols] = jnp.where(left, acc[0], acc[1]) + gain[:, cols] * grad
+        return carry
+
+    lax.fori_loop(0, pairs, back_pair, 0)
+
+    def ecopy(e, f, r, slot):
+        k = peer(r)
+        src, dst = (fbuf, rf) if f == 0 else (sb, rr)
+        return pltpu.make_async_remote_copy(
+            src_ref=src.at[e, k], dst_ref=dst.at[e, slot],
+            send_sem=esend.at[e, f, r], recv_sem=erecv.at[e, f, slot],
+            device_id={"seq": k}, device_id_type=pl.DeviceIdType.MESH)
+
+    def e_start(e, f):
+        for r in range(1, SEQ):
+            ecopy(e, f, r, s).start()
+        if f == 0:
+            rf[e, s] = fbuf[e, s]
+        else:
+            rr[e, s] = sb[e, s]
+
+    def e_wait(e, f):
+        for r in range(1, SEQ):
+            ecopy(e, f, r, peer(r)).wait_recv()
+
+    def fresh(e, src, maps):
+        def one(j, carry):
+            cols = pl.ds(pl.multiple_of(j * 256, 256), 256)
+            fbuf[e, j] = dot_tn(src[:, cols], maps[j // (SEQ // b2.shape[0])]).astype(BF16)
+            return carry
+
+        lax.fori_loop(0, SEQ, one, 0)
+
+    def scan_states(e, order):
+        per = heads // SEQ
+        run = [jnp.zeros((HEAD_DIM, STATE), F32) for _ in range(per)]
+        for k in order:
+            decay = jnp.exp(rt[k])
+            for m in range(per):
+                rows = slice(m * HEAD_DIM, (m + 1) * HEAD_DIM)
+                sb[e, k, rows, :] = run[m].astype(BF16)
+                run[m] = run[m] * decay[m:m + 1, :] + rf[e, k, rows, :].astype(F32)
+
+    def x_part(first, count):
+        def one(i, carry):
+            slot, h = i // 2, i % 2
+            start = peer_dyn(slot) * 2 * half + h * half
+            a = inputs[:, pl.ds(pl.multiple_of(start, 256), half)]
+            for q in range(4):
+                cs = slice(q * 512, (q + 1) * 512)
+                xacc[:, cs] += dot_nn(a, wbuf[slot, h, :, cs])
+            return carry
+
+        lax.fori_loop(first, first + count, one, 0)
+
+    def rcopy(i, src_z, target):
+        slot, h = i // 2, i % 2
+        piece = (peer_dyn(slot) % 2) * 2 + h
+        return pltpu.make_async_remote_copy(
+            src_ref=pbuf.at[i], dst_ref=rsbuf.at[src_z, piece],
+            send_sem=rsend.at[i], recv_sem=rrecv.at[src_z, piece],
+            device_id={"head": target}, device_id_type=pl.DeviceIdType.MESH)
+
+    def p_part(first, count):
+        def one(i, carry):
+            slot, h = i // 2, i % 2
+            owner = peer_dyn(slot)
+            part = dot_nt(xg16[...], wbuf[slot, h]).astype(BF16)
+            target = owner // 2
+
+            @pl.when(target == z)
+            def _():
+                rsbuf[z, (owner % 2) * 2 + h] = part
+
+            @pl.when(target != z)
+            def _():
+                pbuf[i] = part
+                rcopy(i, z, target).start()
+
+            return carry
+
+        lax.fori_loop(first, first + count, one, 0)
+
+    fresh(0, ysc, c2)
+    e_start(0, 0)
+    own.wait()
+    x_part(0, 2)
+    for r in range(1, SEQ):
+        tcopy(r, peer(r)).wait_recv()
+    e_wait(0, 0)
+    scan_states(0, range(SEQ - 1, -1, -1))
+    e_start(0, 1)
+    w_wait(1, 0, 1)
+    w_wait(1, 1, 1)
+    x_part(2, 2)
+    e_wait(0, 1)
+
+    def back_finish(i, carry):
+        cols = columns_of(i)
+        state = rr[0, i // 2, pl.ds(pl.multiple_of((i % 2) * 128, 128), 128), :]
+        pe = pexp[i]
+        tail = jnp.exp(pe[SPAN - 1:SPAN, :] - pe)
+        xg16[:, cols] = (xg[:, cols] + tail * dot_nt(b2[i // per_group], state)).astype(BF16)
+        return carry
+
+    lax.fori_loop(0, pairs, back_finish, 0)
+    w_wait(2, 0, 2)
+    go_send(2, 6, 0, 4)
+    go_send(2, 3, 0, 1)
+    w_wait(4, 1, 4)
+    go_send(4, 6, 1, 2)
+    go_send(4, 5, 1, 1)
+    p_part(0, 4)
+    w_wait(2, 1, 2)
+    go_send(2, 3, 1, 1)
+    w_wait(4, 0, 4)
+    go_send(4, 5, 0, 1)
+    x_part(4, 2)
+    p_part(4, 2)
+    x_part(8, 2)
+    p_part(8, 2)
+    for h in range(2):
+        w_wait(3, h, 1)
+        w_wait(5, h, 1)
+    x_part(6, 2)
+    p_part(6, 2)
+    x_part(10, 2)
+    p_part(10, 2)
+    w_wait(6, 0, 4)
+    go_send(6, 7, 0, 1)
+    w_wait(6, 1, 2)
+    go_send(6, 7, 1, 1)
+    x_part(12, 2)
+    w_wait(7, 0, 1)
+    w_wait(7, 1, 1)
+    x_part(14, 2)
+
+    def fore_scale(i, carry):
+        cols = columns_of(i)
+        x = xacc[:, cols].astype(BF16)
+        x16[:, cols] = x
+        pe = pexp[i]
+        ysc[:, cols] = (x.astype(F32) * jnp.exp(pe[SPAN - 1:SPAN, :] - pe)).astype(BF16)
+        return carry
+
+    lax.fori_loop(0, pairs, fore_scale, 0)
+    fresh(1, ysc, b2)
+    e_start(1, 0)
+    p_part(12, 4)
+    e_wait(1, 0)
+    scan_states(1, range(SEQ))
+    e_start(1, 1)
+
+    def fore_local(i, carry):
+        cols = columns_of(i)
+        x = x16[:, cols]
+        y = jnp.where(left, dot_nn(wts[2 * i], x), dot_nn(wts[2 * i + 1], x))
+        xacc[:, cols] = y + gain[:, cols] * x.astype(F32)
+        return carry
+
+    lax.fori_loop(0, pairs, fore_local, 0)
+    e_wait(1, 1)
+
+    def fore_finish(i, carry):
+        cols = columns_of(i)
+        state = rr[1, i // 2, pl.ds(pl.multiple_of((i % 2) * 128, 128), 128), :]
+        y = xacc[:, cols] + jnp.exp(pexp[i]) * dot_nt(c2[i // per_group], state)
+        gate = gz[:, cols].astype(F32)
+        up = go[:, cols].astype(F32)
+        sigma = jax.nn.sigmoid(gate)
+        zg_ref[:, cols] = (up * y * sigma * (1.0 + gate * (1.0 - sigma))).astype(BF16)
+        return carry
+
+    lax.fori_loop(0, pairs, fore_finish, 0)
+
+    for dz in range(1, RUNS):
+        source = (z + dz) % RUNS
+        for piece in range(4):
+            pltpu.make_async_remote_copy(
+                src_ref=pbuf.at[0], dst_ref=rsbuf.at[source, piece],
+                send_sem=rsend.at[0], recv_sem=rrecv.at[source, piece],
+                device_id={"head": source}, device_id_type=pl.DeviceIdType.MESH).wait_recv()
+    for piece in range(4):
+        total = rsbuf[0, piece].astype(F32)
+        for k in range(1, RUNS):
+            total = total + rsbuf[k, piece].astype(F32)
+        out_ref[:, piece * 256:(piece + 1) * 256] = total.astype(BF16)
+
+    def drain(i, carry):
+        @pl.when(peer_dyn(i // 2) // 2 != z)
+        def _():
+            rcopy(i, z, peer_dyn(i // 2) // 2).wait_send()
+
+        return carry
+
+    lax.fori_loop(0, 16, drain, 0)
+    for cp in sent:
+        cp.wait_send()
+    for r in range(1, SEQ):
+        tcopy(r, s).wait_send()
+        for e in range(2):
+            for f in range(2):
+                ecopy(e, f, r, s).wait_send()
+
+
+def fused_body(inputs, x_weight, b_values, c_values, gate_z, log_decay, skip_gain, grad_out):
+    heads = log_decay.shape[1]
+    width = x_weight.shape[1]
+    depth = x_weight.shape[0]
+    pairs = heads // 2
+    groups = heads * GROUPS // HEADS
+    z = lax.axis_index("head")
+    b2 = jnp.swapaxes(lax.dynamic_slice_in_dim(b_values, z * groups, groups, 1), 0, 1)
+    c2 = jnp.swapaxes(lax.dynamic_slice_in_dim(c_values, z * groups, groups, 1), 0, 1)
+    prefix = jnp.cumsum(log_decay, axis=0)
+    prow = prefix.T.reshape(pairs, 2, SPAN)
+    pexp = jnp.broadcast_to(prow.swapaxes(1, 2)[..., None], (pairs, SPAN, 2, HEAD_DIM)).reshape(pairs, SPAN, 128)
+    totals = prefix[-1].reshape(SEQ, 1, heads // SEQ)
+    tt = jnp.broadcast_to(totals, (SEQ, 8 * SEQ // heads, heads // SEQ)).reshape(SEQ, 8, 1)
+    tt = jnp.broadcast_to(tt, (SEQ, 8, 128))
+    gain = jnp.repeat(skip_gain, HEAD_DIM)[None, :]
+    halves = x_weight.reshape(2, depth // 2, width)
+    vmem = pl.BlockSpec(memory_space=pltpu.VMEM)
+    tokens = inputs.shape[0]
+    dma = pltpu.SemaphoreType.DMA
+    state = (2, SEQ, heads // SEQ * HEAD_DIM, STATE)
+    return tuple(pl.pallas_call(
+        mixer_kernel,
+        out_shape=(
+            jax.ShapeDtypeStruct((tokens, inputs.shape[1] // RUNS), BF16),
+            jax.ShapeDtypeStruct((tokens, width), BF16),
+        ),
+        in_specs=[vmem, pl.BlockSpec(memory_space=pl.ANY)] + [vmem] * 8,
+        out_specs=(vmem, vmem),
+        scratch_shapes=[
+            pltpu.VMEM((SEQ, 2, depth // 2, width), BF16),
+            pltpu.VMEM((tokens, width), F32),
+            pltpu.VMEM((tokens, width), F32),
+            pltpu.VMEM((tokens, width), BF16),
+            pltpu.VMEM((tokens, width), BF16),
+            pltpu.VMEM((heads, SPAN, SPAN), BF16),
+            pltpu.VMEM((groups, SPAN, SPAN), F32),
+            pltpu.VMEM((tokens, width), BF16),
+            pltpu.VMEM((2 * SEQ, tokens, depth // 2), BF16),
+            pltpu.VMEM((RUNS, 4, tokens, depth // 2), BF16),
+            pltpu.VMEM(state, BF16),
+            pltpu.VMEM(state, BF16),
+            pltpu.VMEM(state, BF16),
+            pltpu.VMEM(state, BF16),
+            pltpu.VMEM((SEQ, 8, 128), F32),
+            dma((SEQ, 2)), dma((SEQ, 2)), dma,
+            dma((SEQ,)), dma((SEQ,)),
+            dma((2, 2, SEQ)), dma((2, 2, SEQ)),
+            dma((2 * SEQ,)), dma((RUNS, 4)),
+        ],
+        compiler_params=pltpu.CompilerParams(
+            collective_id=0, has_side_effects=True, vmem_limit_bytes=60 * 1024 * 1024),
+        name="mixer",
+    )(inputs, halves, b2, c2, gate_z, grad_out, pexp, prow, gain, tt))
+
+
 def solution(mesh):
     in_specs = (
         P("seq", None),
@@ -175,4 +552,6 @@
         P("seq", "head"),
     )
     out_specs = (P("seq", "head"), P("seq", "head"))
-    return jax.shard_map(body, mesh=mesh, in_specs=in_specs, out_specs=out_specs, check_vma=False)
+    small = mesh.shape["seq"] == SEQ and mesh.shape["head"] == RUNS
+    chosen = fused_body if small else body
+    return jax.shard_map(chosen, mesh=mesh, in_specs=in_specs, out_specs=out_specs, check_vma=False)

time: 325 us -> 153 us (0.47)
  waiting for transfers between devices: 189 us -> 0 us
  Pallas kernels: 0 us -> 138 us
  matrix products: 57.6 us -> 0 us
  other arithmetic: 25.4 us -> 0.77 us
  blocking collectives: 17.8 us -> 0 us
  between operations: 14 us -> 0.71 us
  local copies, waits for them, and re-layouts: 17.1 us -> 11.2 us
    all_gather x3 -> x0, waiting for transfers between devices: 145 us -> none  [the longest x1 89 us: body(): full_weight = lax.all_gather(x_weight, 'seq', axis=0, tiled=True)]
    pallas_call x0 -> x1, Pallas kernels: none -> 138 us  [fused_body(): pl.pallas_call(mixer_kernel, out_shape=(jax.ShapeDtypeStruct((tokens, inp...]
    dot_general x11 -> x0, matrix products: 57.6 us -> none  [the longest x1 12.1 us: body(): jnp.einsum('tk,dk->td', x_grad, full_weight, preferred_element_type=jnp.f...]
    reduce_scatter x1 -> x0, waiting for transfers between devices: 43.4 us -> none  [body(): lax.psum_scatter(partial_sums.astype(jnp.bfloat16), 'head', scatter_dimen...]
    select_n x16 -> x0, other arithmetic: 20.7 us -> none  [the longest x8 10.4 us: prefix_hop(): return jax.tree.map(lambda a, b: jnp.where(reached, a, b), new, before)]
    all_gather x2 -> x0, blocking collectives: 17.8 us -> none  [the longest x1 8.93 us: entering(): pieces = jax.tree.map(lambda part: lax.all_gather(part, axis), value)]
    rev x2 -> x0, local copies, waits for them, and re-layouts: 8.28 us -> none  [entering(): pieces = jax.tree.map(lambda part: part[::-1], pieces)]
    convert_element_type x10 -> x0, other arithmetic: 3.94 us -> none  [the longest x1 3.88 us: body(): (upstream * outputs * sigma * (1.0 + gate * (1.0 - sigma))).astype(jnp.bf...]
  transfers between devices with their start and end apart: 4 -> 0, of which waited for: 4 -> 0; matrix products, arithmetic and copies ran while one was open for 6% -> 0% of each run, Pallas kernels for 0% -> 0%
where the time goes in v1:
time: 153 us; the launch traced here: 150 us
  Pallas kernels  138 us (90%)
  local copies, waits for them, and re-layouts  11.2 us (7%)
    pallas_call x1, Pallas kernels, fused_body(): pl.pallas_call(mixer_kernel, out_shape=(jax.ShapeDtypeStruct((tokens, inp...  138 us
    unnamed x10, local copies, waits for them, and re-layouts  5.54 us

profile of v1, /device:TPU:16, one launch (start us, length us, event | category | flops | bytes accessed | tf_op | source)
XLA Modules:
  0.0 150.2 jit_solution(15904266406699165697)
XLA Ops:
  0.6 0.0 copy-start
  0.6 1.5 constant_dynamic-slice_fusion
  2.1 0.7 copy.33
  2.8 0.7 copy.34
  3.5 0.0 copy-done
  3.5 0.6 reduce-window.6
  4.1 0.2 slice_reduce_fusion
  4.3 0.1 broadcast_add_fusion
  4.4 0.0 copy-start.1
  4.5 0.2 broadcast_in_dim.23
  4.6 0.0 copy-start.2
  4.6 1.9 %copy.24.pexp = f32[16,256,128]{2,1,0:T(8,128)} copy(f32[16,256,128]{1,2,0:T(8,128)S(1)} %bitcast.23) | data formatting | bytes 4194304 | tf_op jit(solution)/shard_map/reshape | solution.py:498
  6.5 0.0 copy-done.1
  6.5 0.1 bitcast_bitcast_fusion
  6.6 0.2 slice_reduce_fusion.1
  6.8 0.1 broadcast_in_dim.25
  6.8 0.1 copy.22
  6.9 0.1 copy.23
  7.0 0.7 broadcast_in_dim.28.tt
  7.7 0.0 copy-done.2
  7.7 0.1 broadcast_in_dim.24
  7.8 0.7 broadcast_in_dim_reshape.3.gain
  8.5 137.6 %mixer.1 = (bf16[256,1024]{1,0:T(8,128)(2,1)}, bf16[256,2048]{1,0:T(8,128)(2,1)}) custom-call(bf16[256,4096]{1,0:T(8,128)(2,1)} %inputs.1, bf16[2,256,2048]{2,1,0:T(8,128)(2,1)} %bitcast.24, bf16[2,256,128]{2,1,0:T(8,128)(2,1)} %bitcast.26, bf16[2,256,128]{2,1,0:T(8,128)(2,1)} %bitcast.25, bf16[256,2048]{1,0:T(8,128)(2,1)} %gz.1, bf16[256,2048]{1,0:T(8,128)(2,1)} %go.1, ...), custom_call_target="tpu_custom_call" | custom-call | tf_op jit(solution)/shard_map/mixer/pallas_call | solution.py:508
  146.0 1.9 %copy.37 = bf16[256,1024]{1,0:T(8,128)(2,1)} copy(bf16[256,1024]{1,0:T(8,128)(2,1)} %get-tuple-element.6) | data formatting | bytes 1048576
  147.9 2.3 %copy.38 = bf16[256,2048]{1,0:T(8,128)(2,1)} copy(bf16[256,2048]{1,0:T(8,128)(2,1)} %get-tuple-element.7) | data formatting | bytes 2097152
  (6 shorter events, 0.1 us)
Async XLA Ops:
  0.6 2.9 %copy-start = (f32[256,32]{0,1:T(8,128)S(1)}, f32[256,32]{0,1:T(8,128)}, u32[]{:S(2)}) copy-start(f32[256,32]{0,1:T(8,128)} %param.13) | copy-start | bytes 98308
  4.4 2.1 %copy-start.1 = (f32[16,2,256]{2,1,0:T(2,128)}, f32[16,2,256]{2,1,0:T(2,128)S(1)}, u32[]{:S(2)}) copy-start(f32[16,2,256]{2,1,0:T(2,128)S(1)} %reduce_window_sum.20.prow) | copy-start | bytes 98308
  4.6 3.1 %copy-start.2 = (f32[32]{0:T(128)S(1)}, f32[32]{0:T(128)}, u32[]{:S(2)}) copy-start(f32[32]{0:T(128)} %param.14) | copy-start | bytes 388

commit v2 on v1

--- a/solution.py
+++ b/solution.py
@@ -184,11 +184,12 @@
 
 
 def mixer_kernel(
-    inputs, w_hbm, b2, c2, gz, go, pexp, prow, gain, tt,
+    in_hbm, w_hbm, b_flat, c_flat, gz_hbm, go_hbm, decay_ref, skip_ref,
     out_ref, zg_ref,
-    wbuf, xacc, xg, xg16, ysc, wts, gmat, x16, pbuf, rsbuf,
+    inputs, gz, go, b2, c2, pexp, prow, gain, tt,
+    wbuf, xacc, xg, xg16, ysc, wts, gmat, x16, pbuf, rin,
     fbuf, rf, sb, rr, rt,
-    wsend, wrecv, wlocal, tsend, trecv, esend, erecv, rsend, rrecv,
+    loads, wsend, wrecv, wlocal, tsend, trecv, esend, erecv, rsend, rrecv,
 ):
     s = lax.axis_index("seq")
     z = lax.axis_index("head")
@@ -210,6 +211,10 @@
         c = (yy + r // 4) % 2
         return c * 4 + b * 2 + a
 
+    staged = [pltpu.make_async_copy(src, dst, loads.at[n]) for n, (src, dst) in enumerate(
+        ((gz_hbm, gz), (go_hbm, go), (in_hbm, inputs)))]
+    for cp in staged:
+        cp.start()
     barrier = pltpu.get_barrier_semaphore()
     for r in range(1, SEQ):
         pl.semaphore_signal(barrier, inc=1, device_id={"seq": peer(r)}, device_id_type=pl.DeviceIdType.MESH)
@@ -241,8 +246,6 @@
             src_ref=tt.at[k], dst_ref=rt.at[slot], send_sem=tsend.at[r], recv_sem=trecv.at[slot],
             device_id={"seq": k}, device_id_type=pl.DeviceIdType.MESH)
 
-    for r in range(1, SEQ):
-        tcopy(r, s).start()
     go_send(0, 2, 0, 2)
     go_send(0, 4, 1, 4)
     go_send(0, 2, 1, 2)
@@ -251,8 +254,40 @@
     go_send(0, 1, 0, 1)
     go_send(0, 1, 1, 1)
 
+    groups = b2.shape[0]
+    for g in range(groups):
+        span = pl.ds(pl.multiple_of((z * groups + g) * STATE, STATE), STATE)
+        b2[g] = b_flat[:, span]
+        c2[g] = c_flat[:, span]
+    lower = (lax.broadcasted_iota(jnp.int32, (SPAN, SPAN), 0) >= lax.broadcasted_iota(jnp.int32, (SPAN, SPAN), 1))
+    ones = jnp.where(lower, 1.0, 0.0).astype(F32)
+    prefix = lax.dot_general(ones, decay_ref[...], (((1,), (0,)), ((), ())), preferred_element_type=F32, precision=EXACT_MODE)
+    across = lax.dot_general(decay_ref[...], ones, (((0,), (1,)), ((), ())), preferred_element_type=F32, precision=EXACT_MODE)
+    per_chunk = heads // SEQ
+    closing = jnp.broadcast_to(across[:, SPAN - 1:SPAN], (heads, 128))
+    tt[...] = jnp.zeros_like(tt)
+    for j in range(SEQ):
+        tt[j, 0:per_chunk, :] = closing[j * per_chunk:(j + 1) * per_chunk, :]
+    for i in range(pairs):
+        prow[i, 0:2, :] = across[2 * i:2 * i + 2, :]
+    both = jnp.concatenate([prefix, jnp.broadcast_to(skip_ref[...], (8, heads))], axis=0)
+
+    def expand_pair(i, carry):
+        head = lax.broadcasted_iota(jnp.int32, (heads, 128), 0)
+        lane = lax.broadcasted_iota(jnp.int32, (heads, 128), 1)
+        pick = jnp.where(head == 2 * i + lane // HEAD_DIM, 1.0, 0.0).astype(F32)
+        wide = lax.dot_general(both, pick, (((1,), (0,)), ((), ())), preferred_element_type=F32, precision=EXACT_MODE)
+        pexp[i] = wide[:SPAN]
+        gain[i] = wide[SPAN:]
+        return carry
+
+    lax.fori_loop(0, pairs, expand_pair, 0)
     rt[s] = tt[s]
-    for g in range(b2.shape[0]):
+    for r in range(1, SEQ):
+        tcopy(r, s).start()
+    staged[0].wait()
+    staged[1].wait()
+    for g in range(groups):
         gmat[g] = dot_nt(c2[g], b2[g])
     xacc[...] = jnp.zeros_like(xacc)
     lanes = lax.broadcasted_iota(jnp.int32, (SPAN, 128), 1)
@@ -279,7 +314,7 @@
             w = (scores * factors).astype(BF16)
             wts[2 * i + k] = w
             acc.append(dot_tn(w, low))
-        xg[:, cols] = jnp.where(left, acc[0], acc[1]) + gain[:, cols] * grad
+        xg[:, cols] = jnp.where(left, acc[0], acc[1]) + gain[i, 0:1, :] * grad
         return carry
 
     lax.fori_loop(0, pairs, back_pair, 0)
@@ -334,29 +369,40 @@
 
         lax.fori_loop(first, first + count, one, 0)
 
-    def rcopy(i, src_z, target):
-        slot, h = i // 2, i % 2
-        piece = (peer_dyn(slot) % 2) * 2 + h
+    def route(i):
+        target = peer_dyn(i // 2) // 2
+        up = (z + RUNS - 1 - target) // RUNS
+        return target, up, up * (RUNS - 1)
+
+    def rcopy(i, up):
         return pltpu.make_async_remote_copy(
-            src_ref=pbuf.at[i], dst_ref=rsbuf.at[src_z, piece],
-            send_sem=rsend.at[i], recv_sem=rrecv.at[src_z, piece],
-            device_id={"head": target}, device_id_type=pl.DeviceIdType.MESH)
+            src_ref=pbuf.at[i], dst_ref=rin.at[up, i],
+            send_sem=rsend.at[i], recv_sem=rrecv.at[up, i],
+            device_id={"head": (z + 1 + up * 2) % RUNS}, device_id_type=pl.DeviceIdType.MESH)
 
     def p_part(first, count):
         def one(i, carry):
             slot, h = i // 2, i % 2
-            owner = peer_dyn(slot)
-            part = dot_nt(xg16[...], wbuf[slot, h]).astype(BF16)
-            target = owner // 2
-
-            @pl.when(target == z)
+            target, up, edge = route(i)
+            pbuf[i] = dot_nt(xg16[...], wbuf[slot, h]).astype(BF16)
+
+            @pl.when((target != z) & (z == edge))
             def _():
-                rsbuf[z, (owner % 2) * 2 + h] = part
-
-            @pl.when(target != z)
+                rcopy(i, up).start()
+
+            return carry
+
+        lax.fori_loop(first, first + count, one, 0)
+
+    def p_pass(first, count):
+        def one(i, carry):
+            target, up, edge = route(i)
+
+            @pl.when((target != z) & (z != edge))
             def _():
-                pbuf[i] = part
-                rcopy(i, z, target).start()
+                rcopy(i, up).wait_recv()
+                pbuf[i] = (pbuf[i].astype(F32) + rin[up, i].astype(F32)).astype(BF16)
+                rcopy(i, up).start()
 
             return carry
 
@@ -365,6 +411,7 @@
     fresh(0, ysc, c2)
     e_start(0, 0)
     own.wait()
+    staged[2].wait()
     x_part(0, 2)
     for r in range(1, SEQ):
         tcopy(r, peer(r)).wait_recv()
@@ -400,6 +447,7 @@
     p_part(4, 2)
     x_part(8, 2)
     p_part(8, 2)
+    p_pass(0, 4)
     for h in range(2):
         w_wait(3, h, 1)
         w_wait(5, h, 1)
@@ -412,6 +460,7 @@
     w_wait(6, 1, 2)
     go_send(6, 7, 1, 1)
     x_part(12, 2)
+    p_pass(4, 8)
     w_wait(7, 0, 1)
     w_wait(7, 1, 1)
     x_part(14, 2)
@@ -431,12 +480,13 @@
     e_wait(1, 0)
     scan_states(1, range(SEQ))
     e_start(1, 1)
+    p_pass(12, 4)
 
     def fore_local(i, carry):
         cols = columns_of(i)
         x = x16[:, cols]
         y = jnp.where(left, dot_nn(wts[2 * i], x), dot_nn(wts[2 * i + 1], x))
-        xacc[:, cols] = y + gain[:, cols] * x.astype(F32)
+        xacc[:, cols] = y + gain[i, 0:1, :] * x.astype(F32)
         return carry
 
     lax.fori_loop(0, pairs, fore_local, 0)
@@ -454,23 +504,37 @@
 
     lax.fori_loop(0, pairs, fore_finish, 0)
 
-    for dz in range(1, RUNS):
-        source = (z + dz) % RUNS
-        for piece in range(4):
-            pltpu.make_async_remote_copy(
-                src_ref=pbuf.at[0], dst_ref=rsbuf.at[source, piece],
-                send_sem=rsend.at[0], recv_sem=rrecv.at[source, piece],
-                device_id={"head": source}, device_id_type=pl.DeviceIdType.MESH).wait_recv()
-    for piece in range(4):
-        total = rsbuf[0, piece].astype(F32)
-        for k in range(1, RUNS):
-            total = total + rsbuf[k, piece].astype(F32)
-        out_ref[:, piece * 256:(piece + 1) * 256] = total.astype(BF16)
+    def gather_own(i, carry):
+        owner = peer_dyn(i // 2)
+
+        @pl.when(owner // 2 == z)
+        def _():
+            piece = (owner % 2) * 2 + i % 2
+            out_cols = pl.ds(pl.multiple_of(piece * 256, 256), 256)
+            xg[:, out_cols] = pbuf[i].astype(F32)
+
+            @pl.when(z != 0)
+            def _():
+                rcopy(i, 0).wait_recv()
+                xg[:, out_cols] += rin[0, i].astype(F32)
+
+            @pl.when(z != RUNS - 1)
+            def _():
+                rcopy(i, 1).wait_recv()
+                xg[:, out_cols] += rin[1, i].astype(F32)
+
+            out_ref[:, out_cols] = xg[:, out_cols].astype(BF16)
+
+        return carry
+
+    lax.fori_loop(0, 16, gather_own, 0)
 
     def drain(i, carry):
-        @pl.when(peer_dyn(i // 2) // 2 != z)
+        target, up, edge = route(i)
+
+        @pl.when(target != z)
         def _():
-            rcopy(i, z, peer_dyn(i // 2) // 2).wait_send()
+            rcopy(i, up).wait_send()
 
         return carry
 
@@ -490,18 +554,11 @@
     depth = x_weight.shape[0]
     pairs = heads // 2
     groups = heads * GROUPS // HEADS
-    z = lax.axis_index("head")
-    b2 = jnp.swapaxes(lax.dynamic_slice_in_dim(b_values, z * groups, groups, 1), 0, 1)
-    c2 = jnp.swapaxes(lax.dynamic_slice_in_dim(c_values, z * groups, groups, 1), 0, 1)
-    prefix = jnp.cumsum(log_decay, axis=0)
-    prow = prefix.T.reshape(pairs, 2, SPAN)
-    pexp = jnp.broadcast_to(prow.swapaxes(1, 2)[..., None], (pairs, SPAN, 2, HEAD_DIM)).reshape(pairs, SPAN, 128)
-    totals = prefix[-1].reshape(SEQ, 1, heads // SEQ)
-    tt = jnp.broadcast_to(totals, (SEQ, 8 * SEQ // heads, heads // SEQ)).reshape(SEQ, 8, 1)
-    tt = jnp.broadcast_to(tt, (SEQ, 8, 128))
-    gain = jnp.repeat(skip_gain, HEAD_DIM)[None, :]
+    b_flat = b_values.reshape(b_values.shape[0], GROUPS * STATE)
+    c_flat = c_values.reshape(c_values.shape[0], GROUPS * STATE)
     halves = x_weight.reshape(2, depth // 2, width)
     vmem = pl.BlockSpec(memory_space=pltpu.VMEM)
+    hbm = pl.BlockSpec(memory_space=pl.ANY)
     tokens = inputs.shape[0]
     dma = pltpu.SemaphoreType.DMA
     state = (2, SEQ, heads // SEQ * HEAD_DIM, STATE)
@@ -511,9 +568,18 @@
             jax.ShapeDtypeStruct((tokens, inputs.shape[1] // RUNS), BF16),
             jax.ShapeDtypeStruct((tokens, width), BF16),
         ),
-        in_specs=[vmem, pl.BlockSpec(memory_space=pl.ANY)] + [vmem] * 8,
+        in_specs=[hbm, hbm, vmem, vmem, hbm, hbm, vmem, vmem],
         out_specs=(vmem, vmem),
         scratch_shapes=[
+            pltpu.VMEM(inputs.shape, BF16),
+            pltpu.VMEM((tokens, width), BF16),
+            pltpu.VMEM((tokens, width), BF16),
+            pltpu.VMEM((groups, SPAN, STATE), BF16),
+            pltpu.VMEM((groups, SPAN, STATE), BF16),
+            pltpu.VMEM((pairs, SPAN, 128), F32),
+            pltpu.VMEM((pairs, 8, SPAN), F32),
+            pltpu.VMEM((pairs, 8, 128), F32),
+            pltpu.VMEM((SEQ, 8, 128), F32),
             pltpu.VMEM((SEQ, 2, depth // 2, width), BF16),
             pltpu.VMEM((tokens, width), F32),
             pltpu.VMEM((tokens, width), F32),
@@ -523,21 +589,21 @@
             pltpu.VMEM((groups, SPAN, SPAN), F32),
             pltpu.VMEM((tokens, width), BF16),
             pltpu.VMEM((2 * SEQ, tokens, depth // 2), BF16),
-            pltpu.VMEM((RUNS, 4, tokens, depth // 2), BF16),
+            pltpu.VMEM((2, 2 * SEQ, tokens, depth // 2), BF16),
             pltpu.VMEM(state, BF16),
             pltpu.VMEM(state, BF16),
             pltpu.VMEM(state, BF16),
             pltpu.VMEM(state, BF16),
             pltpu.VMEM((SEQ, 8, 128), F32),
-            dma((SEQ, 2)), dma((SEQ, 2)), dma,
+            dma((3,)), dma((SEQ, 2)), dma((SEQ, 2)), dma,
             dma((SEQ,)), dma((SEQ,)),
             dma((2, 2, SEQ)), dma((2, 2, SEQ)),
-            dma((2 * SEQ,)), dma((RUNS, 4)),
+            dma((2 * SEQ,)), dma((2, 2 * SEQ)),
         ],
         compiler_params=pltpu.CompilerParams(
             collective_id=0, has_side_effects=True, vmem_limit_bytes=60 * 1024 * 1024),
         name="mixer",
-    )(inputs, halves, b2, c2, gate_z, grad_out, pexp, prow, gain, tt))
+    )(inputs, halves, b_flat, c_flat, gate_z, grad_out, log_decay, skip_gain[None, :]))
 
 
 def solution(mesh):

time: 153 us -> 159 us (1.039); the launches traced: 150 us -> 158 us
  Pallas kernels: 138 us -> 149 us
  local copies, waits for them, and re-layouts: 11.2 us -> 8.06 us
    pallas_call x1, Pallas kernels: 138 us -> 149 us  [fused_body(): pl.pallas_call(mixer_kernel, out_shape=(jax.ShapeDtypeStruct((tokens, inp...]
    unnamed x10 -> x3, local copies, waits for them, and re-layouts: 5.54 us -> 5.68 us
where the time goes in v2:
time: 159 us; the launch traced here: 158 us
  Pallas kernels  149 us (94%)
  local copies, waits for them, and re-layouts  8.06 us (5%)
    pallas_call x1, Pallas kernels, fused_body(): pl.pallas_call(mixer_kernel, out_shape=(jax.ShapeDtypeStruct((tokens, inp...  149 us
    unnamed x3, local copies, waits for them, and re-layouts  5.68 us

profile of v2, /device:TPU:16, one launch (start us, length us, event | category | flops | bytes accessed | tf_op | source)
XLA Modules:
  0.0 158.0 jit_solution(3273078501233387496)
XLA Ops:
  0.6 1.5 copy.10.decay_ref
  2.1 2.4 %copy_bitcast_fusion = (bf16[256,1024]{1,0:T(8,128)(2,1)}, bf16[256,1024]{1,0:T(8,128)(2,1)}) fusion(bf16[32,8,8,128]{3,2,1,0:T(8,128)(2,1)} %bitcast.9, bf16[32,8,8,128]{3,2,1,0:T(8,128)(2,1)} %bitcast.10), kind=kLoop, calls=%fused_computation | loop fusion | bytes 2097152 | tf_op jit(solution)/shard_map/reshape | solution.py:558
  4.5 149.3 %mixer.1 = (bf16[256,1024]{1,0:T(8,128)(2,1)}, bf16[256,2048]{1,0:T(8,128)(2,1)}) custom-call(bf16[256,4096]{1,0:T(8,128)(2,1)} %in_hbm.1, bf16[2,256,2048]{2,1,0:T(8,128)(2,1)} %bitcast.8, bf16[256,1024]{1,0:T(8,128)(2,1)} %get-tuple-element.3.b_flat, bf16[256,1024]{1,0:T(8,128)(2,1)} %get-tuple-element.2.c_flat, bf16[256,2048]{1,0:T(8,128)(2,1)} %gz_hbm.1, ...), custom_call_target="tpu_custom_call" | custom-call | tf_op jit(solution)/shard_map/mixer/pallas_call | solution.py:565
  153.8 1.9 %copy.17 = bf16[256,1024]{1,0:T(8,128)(2,1)} copy(bf16[256,1024]{1,0:T(8,128)(2,1)} %get-tuple-element.6) | data formatting | bytes 1048576
  155.7 2.3 %copy.18 = bf16[256,2048]{1,0:T(8,128)(2,1)} copy(bf16[256,2048]{1,0:T(8,128)(2,1)} %get-tuple-element.7) | data formatting | bytes 2097152

commit v3 on v2

--- a/solution.py
+++ b/solution.py
@@ -187,9 +187,9 @@
     in_hbm, w_hbm, b_flat, c_flat, gz_hbm, go_hbm, decay_ref, skip_ref,
     out_ref, zg_ref,
     inputs, gz, go, b2, c2, pexp, prow, gain, tt,
-    wbuf, xacc, xg, xg16, ysc, wts, gmat, x16, pbuf, rin,
+    wbuf, xacc, xg, xg16, ysc, wts, gmat, x16, pbuf, rin, rdir,
     fbuf, rf, sb, rr, rt,
-    loads, wsend, wrecv, wlocal, tsend, trecv, esend, erecv, rsend, rrecv,
+    loads, wsend, wrecv, wlocal, tsend, trecv, esend, erecv, rsend, rrecv, rdrecv,
 ):
     s = lax.axis_index("seq")
     z = lax.axis_index("head")
@@ -376,19 +376,29 @@
 
     def rcopy(i, up):
         return pltpu.make_async_remote_copy(
-            src_ref=pbuf.at[i], dst_ref=rin.at[up, i],
-            send_sem=rsend.at[i], recv_sem=rrecv.at[up, i],
+            src_ref=pbuf.at[i], dst_ref=rin.at[up, i - 12],
+            send_sem=rsend.at[i], recv_sem=rrecv.at[up, i - 12],
             device_id={"head": (z + 1 + up * 2) % RUNS}, device_id_type=pl.DeviceIdType.MESH)
+
+    def dcopy(i, source, target):
+        return pltpu.make_async_remote_copy(
+            src_ref=pbuf.at[i], dst_ref=rdir.at[source, i % 4],
+            send_sem=rsend.at[i], recv_sem=rdrecv.at[source, i % 4],
+            device_id={"head": target}, device_id_type=pl.DeviceIdType.MESH)
 
     def p_part(first, count):
         def one(i, carry):
             slot, h = i // 2, i % 2
             target, up, edge = route(i)
             pbuf[i] = dot_nt(xg16[...], wbuf[slot, h]).astype(BF16)
-
-            @pl.when((target != z) & (z == edge))
-            def _():
-                rcopy(i, up).start()
+            if first >= 12:
+                @pl.when((target != z) & (z == edge))
+                def _():
+                    rcopy(i, up).start()
+            else:
+                @pl.when(target != z)
+                def _():
+                    dcopy(i, z, target).start()
 
             return carry
 
@@ -401,7 +411,7 @@
             @pl.when((target != z) & (z != edge))
             def _():
                 rcopy(i, up).wait_recv()
-                pbuf[i] = (pbuf[i].astype(F32) + rin[up, i].astype(F32)).astype(BF16)
+                pbuf[i] = (pbuf[i].astype(F32) + rin[up, i - 12].astype(F32)).astype(BF16)
                 rcopy(i, up).start()
 
             return carry
@@ -447,7 +457,6 @@
     p_part(4, 2)
     x_part(8, 2)
     p_part(8, 2)
-    p_pass(0, 4)
     for h in range(2):
         w_wait(3, h, 1)
         w_wait(5, h, 1)
@@ -460,7 +469,7 @@
     w_wait(6, 1, 2)
     go_send(6, 7, 1, 1)
     x_part(12, 2)
-    p_pass(4, 8)
+    p_part(12, 2)
     w_wait(7, 0, 1)
     w_wait(7, 1, 1)
     x_part(14, 2)
@@ -476,11 +485,12 @@
     lax.fori_loop(0, pairs, fore_scale, 0)
     fresh(1, ysc, b2)
     e_start(1, 0)
-    p_part(12, 4)
+    p_part(14, 2)
+    p_pass(12, 2)
     e_wait(1, 0)
     scan_states(1, range(SEQ))
     e_start(1, 1)
-    p_pass(12, 4)
+    p_pass(14, 2)
 
     def fore_local(i, carry):
         cols = columns_of(i)
@@ -504,7 +514,7 @@
 
     lax.fori_loop(0, pairs, fore_finish, 0)
 
-    def gather_own(i, carry):
+    def own_chunk(i, far):
         owner = peer_dyn(i // 2)
 
         @pl.when(owner // 2 == z)
@@ -512,29 +522,40 @@
             piece = (owner % 2) * 2 + i % 2
             out_cols = pl.ds(pl.multiple_of(piece * 256, 256), 256)
             xg[:, out_cols] = pbuf[i].astype(F32)
-
-            @pl.when(z != 0)
-            def _():
-                rcopy(i, 0).wait_recv()
-                xg[:, out_cols] += rin[0, i].astype(F32)
-
-            @pl.when(z != RUNS - 1)
-            def _():
-                rcopy(i, 1).wait_recv()
-                xg[:, out_cols] += rin[1, i].astype(F32)
-
+            if far:
+                @pl.when(z != 0)
+                def _():
+                    rcopy(i, 0).wait_recv()
+                    xg[:, out_cols] += rin[0, i - 12].astype(F32)
+
+                @pl.when(z != RUNS - 1)
+                def _():
+                    rcopy(i, 1).wait_recv()
+                    xg[:, out_cols] += rin[1, i - 12].astype(F32)
+            else:
+                for dz in range(1, RUNS):
+                    source = (z + dz) % RUNS
+                    dcopy(i, source, source).wait_recv()
+                    xg[:, out_cols] += rdir[source, i % 4].astype(F32)
             out_ref[:, out_cols] = xg[:, out_cols].astype(BF16)
 
-        return carry
-
-    lax.fori_loop(0, 16, gather_own, 0)
+    def own_near(i, carry):
+        own_chunk(i, False)
+        return carry
+
+    def own_far(i, carry):
+        own_chunk(i, True)
+        return carry
+
+    lax.fori_loop(0, 12, own_near, 0)
+    lax.fori_loop(12, 16, own_far, 0)
 
     def drain(i, carry):
-        target, up, edge = route(i)
+        target = route(i)[0]
 
         @pl.when(target != z)
         def _():
-            rcopy(i, up).wait_send()
+            dcopy(i, z, target).wait_send()
 
         return carry
 
@@ -589,7 +610,8 @@
             pltpu.VMEM((groups, SPAN, SPAN), F32),
             pltpu.VMEM((tokens, width), BF16),
             pltpu.VMEM((2 * SEQ, tokens, depth // 2), BF16),
-            pltpu.VMEM((2, 2 * SEQ, tokens, depth // 2), BF16),
+            pltpu.VMEM((2, 4, tokens, depth // 2), BF16),
+            pltpu.VMEM((RUNS, 4, tokens, depth // 2), BF16),
             pltpu.VMEM(state, BF16),
             pltpu.VMEM(state, BF16),
             pltpu.VMEM(state, BF16),
@@ -598,7 +620,7 @@
             dma((3,)), dma((SEQ, 2)), dma((SEQ, 2)), dma,
             dma((SEQ,)), dma((SEQ,)),
             dma((2, 2, SEQ)), dma((2, 2, SEQ)),
-            dma((2 * SEQ,)), dma((2, 2 * SEQ)),
+            dma((2 * SEQ,)), dma((2, 4)), dma((RUNS, 4)),
         ],
         compiler_params=pltpu.CompilerParams(
             collective_id=0, has_side_effects=True, vmem_limit_bytes=60 * 1024 * 1024),

time: 159 us -> 135 us (0.85)
  Pallas kernels: 149 us -> 126 us
    pallas_call x1, Pallas kernels: 149 us -> 126 us  [fused_body(): pl.pallas_call(mixer_kernel, out_shape=(jax.ShapeDtypeStruct((tokens, inp...]
where the time goes in v3:
time: 135 us
  Pallas kernels  126 us (93%)
  local copies, waits for them, and re-layouts  8.06 us (6%)
    pallas_call x1, Pallas kernels, fused_body(): pl.pallas_call(mixer_kernel, out_shape=(jax.ShapeDtypeStruct((tokens, inp...  126 us
    unnamed x3, local copies, waits for them, and re-layouts  5.68 us

profile of v3, /device:TPU:16, one launch (start us, length us, event | category | flops | bytes accessed | tf_op | source)
XLA Modules:
  0.0 134.5 jit_solution(11542995707313142816)
XLA Ops:
  0.6 1.5 %copy.10.decay_ref = f32[256,32]{1,0:T(8,128)} copy(f32[256,32]{0,1:T(8,128)} %param.13) | data formatting | bytes 65536 | tf_op args[5]
  2.1 2.4 %copy_bitcast_fusion = (bf16[256,1024]{1,0:T(8,128)(2,1)}, bf16[256,1024]{1,0:T(8,128)(2,1)}) fusion(bf16[32,8,8,128]{3,2,1,0:T(8,128)(2,1)} %bitcast.9, bf16[32,8,8,128]{3,2,1,0:T(8,128)(2,1)} %bitcast.10), kind=kLoop, calls=%fused_computation | loop fusion | bytes 2097152 | tf_op jit(solution)/shard_map/reshape | solution.py:579
  4.5 125.8 %mixer.1 = (bf16[256,1024]{1,0:T(8,128)(2,1)}, bf16[256,2048]{1,0:T(8,128)(2,1)}) custom-call(bf16[256,4096]{1,0:T(8,128)(2,1)} %in_hbm.1, bf16[2,256,2048]{2,1,0:T(8,128)(2,1)} %bitcast.8, bf16[256,1024]{1,0:T(8,128)(2,1)} %get-tuple-element.3.b_flat, bf16[256,1024]{1,0:T(8,128)(2,1)} %get-tuple-element.2.c_flat, bf16[256,2048]{1,0:T(8,128)(2,1)} %gz_hbm.1, ...), custom_call_target="tpu_custom_call" | custom-call | tf_op jit(solution)/shard_map/mixer/pallas_call | solution.py:586
  130.3 1.9 %copy.17 = bf16[256,1024]{1,0:T(8,128)(2,1)} copy(bf16[256,1024]{1,0:T(8,128)(2,1)} %get-tuple-element.6) | data formatting | bytes 1048576
  132.2 2.3 %copy.18 = bf16[256,2048]{1,0:T(8,128)(2,1)} copy(bf16[256,2048]{1,0:T(8,128)(2,1)} %get-tuple-element.7) | data formatting | bytes 2097152

commit v4 on v3

--- a/solution.py
+++ b/solution.py
@@ -431,6 +431,12 @@
     w_wait(1, 0, 1)
     w_wait(1, 1, 1)
     x_part(2, 2)
+    w_wait(2, 0, 2)
+    go_send(2, 6, 0, 4)
+    go_send(2, 3, 0, 1)
+    w_wait(4, 1, 4)
+    go_send(4, 6, 1, 2)
+    go_send(4, 5, 1, 1)
     e_wait(0, 1)
 
     def back_finish(i, carry):
@@ -442,12 +448,6 @@
         return carry
 
     lax.fori_loop(0, pairs, back_finish, 0)
-    w_wait(2, 0, 2)
-    go_send(2, 6, 0, 4)
-    go_send(2, 3, 0, 1)
-    w_wait(4, 1, 4)
-    go_send(4, 6, 1, 2)
-    go_send(4, 5, 1, 1)
     p_part(0, 4)
     w_wait(2, 1, 2)
     go_send(2, 3, 1, 1)

time: 135 us -> 131 us (0.970)
  Pallas kernels: 126 us -> 122 us
    pallas_call x1, Pallas kernels: 126 us -> 122 us  [fused_body(): pl.pallas_call(mixer_kernel, out_shape=(jax.ShapeDtypeStruct((tokens, inp...]
where the time goes in v4:
time: 131 us
  Pallas kernels  122 us (93%)
  local copies, waits for them, and re-layouts  8.06 us (6%)
    pallas_call x1, Pallas kernels, fused_body(): pl.pallas_call(mixer_kernel, out_shape=(jax.ShapeDtypeStruct((tokens, inp...  122 us
    unnamed x3, local copies, waits for them, and re-layouts  5.68 us

profile of v4, /device:TPU:16, one launch (start us, length us, event | category | flops | bytes accessed | tf_op | source)
XLA Modules:
  0.0 130.8 jit_solution(6981477629941905953)
XLA Ops:
  0.6 1.5 %copy.10.decay_ref = f32[256,32]{1,0:T(8,128)} copy(f32[256,32]{0,1:T(8,128)} %param.13) | data formatting | bytes 65536 | tf_op args[5]
  2.1 2.4 %copy_bitcast_fusion = (bf16[256,1024]{1,0:T(8,128)(2,1)}, bf16[256,1024]{1,0:T(8,128)(2,1)}) fusion(bf16[32,8,8,128]{3,2,1,0:T(8,128)(2,1)} %bitcast.9, bf16[32,8,8,128]{3,2,1,0:T(8,128)(2,1)} %bitcast.10), kind=kLoop, calls=%fused_computation | loop fusion | bytes 2097152 | tf_op jit(solution)/shard_map/reshape | solution.py:579
  4.5 122.1 %mixer.1 = (bf16[256,1024]{1,0:T(8,128)(2,1)}, bf16[256,2048]{1,0:T(8,128)(2,1)}) custom-call(bf16[256,4096]{1,0:T(8,128)(2,1)} %in_hbm.1, bf16[2,256,2048]{2,1,0:T(8,128)(2,1)} %bitcast.8, bf16[256,1024]{1,0:T(8,128)(2,1)} %get-tuple-element.3.b_flat, bf16[256,1024]{1,0:T(8,128)(2,1)} %get-tuple-element.2.c_flat, bf16[256,2048]{1,0:T(8,128)(2,1)} %gz_hbm.1, ...), custom_call_target="tpu_custom_call" | custom-call | tf_op jit(solution)/shard_map/mixer/pallas_call | solution.py:586
  126.6 1.9 %copy.17 = bf16[256,1024]{1,0:T(8,128)(2,1)} copy(bf16[256,1024]{1,0:T(8,128)(2,1)} %get-tuple-element.6) | data formatting | bytes 1048576
  128.5 2.3 %copy.18 = bf16[256,2048]{1,0:T(8,128)(2,1)} copy(bf16[256,2048]{1,0:T(8,128)(2,1)} %get-tuple-element.7) | data formatting | bytes 2097152
